TPU v7x, 512 devices: a whole 4x4x16 slice. The times are simulated.
512 devices in a mesh: lat: 4 (over y_hi, core), lon: 128 (over x, z, y_lo).
Axes of the slice: x: 4, y: 4 (y_hi: 2, y_lo: 2; y = y_hi * 2 + y_lo), z: 16, core: 2. Of those that a mesh axis runs over, the one named last changes fastest.
Arguments:
- features: bfloat16 [128, 1024, 1024], P('lat', 'lon'), may hold values from -18 to 18
- depth_kernel: bfloat16 [7, 7, 1024], replicated, may hold values from -0.875 to 0.875
- depth_bias: float32 [1024], replicated, may hold values from -3 to 3
- norm_gain: float32 [1024], replicated, may hold values from 0.1 to 1.9
- norm_bias: float32 [1024], replicated, may hold values from -3 to 3
- up_weight: bfloat16 [1024, 4096], P('lon', 'lat'), may hold values from -0.1875 to 0.1875
- up_bias: float32 [4096], P('lat'), may hold values from -3 to 3
- down_weight: bfloat16 [1024, 4096], P('lon', 'lat'), may hold values from -0.09375 to 0.09375
- down_bias: float32 [1024], replicated, may hold values from -3 to 3
- layer_scale: float32 [1024], replicated, may hold values from 0.3 to 2
Outputs:
- updated: bfloat16 [128, 1024, 1024], P('lat', 'lon')
All inputs are finite; a program needn't handle non-finite values.
Results may differ from a plain program's by a relative error of at most 0.0085.
Values may be sent and summed in bfloat16 or wider, within the bound.
A program may use at most 64 MiB of HBM per device.

v0:
```python
import jax
import jax.numpy as jnp
from jax import lax
from jax.sharding import PartitionSpec as P


def with_halo(block, sides, width, periodic):
    for axis, dim in sides:
        count = lax.axis_size(axis)
        forward = [(i, i + 1) for i in range(count - 1)]
        if periodic:
            forward.append((count - 1, 0))
        backward = [(target, source) for source, target in forward]
        low = lax.ppermute(
            lax.slice_in_dim(block, block.shape[dim] - width, None, axis=dim), axis, forward
        )
        high = lax.ppermute(lax.slice_in_dim(block, 0, width, axis=dim), axis, backward)
        block = jnp.concatenate([low, block, high], axis=dim)
    return block


def local(
    features,
    depth_kernel,
    depth_bias,
    norm_gain,
    norm_bias,
    up_weight,
    up_bias,
    down_weight,
    down_bias,
    layer_scale,
):
    row_count, col_count, chan_count = features.shape
    circled = with_halo(features, (("lon", 1),), 3, True)
    padded = with_halo(circled, (("lat", 0),), 3, False)
    kernel = depth_kernel.astype(jnp.float32)
    total = jnp.zeros((row_count, col_count, chan_count), jnp.float32) + depth_bias
    for row_off in range(7):
        for col_off in range(7):
            window = padded[row_off : row_off + row_count, col_off : col_off + col_count].astype(
                jnp.float32
            )
            total = total + window * kernel[row_off, col_off]
    centre = jnp.mean(total, axis=-1, keepdims=True)
    spread = jnp.mean((total - centre) ** 2, axis=-1, keepdims=True)
    normed = ((total - centre) * lax.rsqrt(spread + 1e-06) * norm_gain + norm_bias).astype(
        jnp.bfloat16
    )
    normed = normed.reshape(row_count * col_count, chan_count)
    gathered = lax.all_gather(normed, "lat", axis=0, tiled=True)
    pre = (
        jnp.dot(
            gathered,
            lax.all_gather(up_weight, "lon", axis=0, tiled=True),
            preferred_element_type=jnp.float32,
        )
        + up_bias
    )
    hidden = jax.nn.gelu(pre, approximate=False).astype(jnp.bfloat16)
    partial_out = lax.dot_general(
        hidden,
        lax.all_gather(down_weight, "lon", axis=0, tiled=True),
        (((1,), (1,)), ((), ())),
        preferred_element_type=jnp.float32,
    )
    branch = lax.psum_scatter(
        partial_out.astype(jnp.bfloat16), "lat", scatter_dimension=0, tiled=True
    ).astype(jnp.float32)
    branch = branch.reshape(row_count, col_count, chan_count)
    updated = features.astype(jnp.float32) + layer_scale * (branch + down_bias)
    return updated.astype(jnp.bfloat16)


def solution(mesh):
    placed = (
        P("lat", "lon", None),
        P(),
        P(),
        P(),
        P(),
        P("lon", "lat"),
        P("lat"),
        P("lon", "lat"),
        P(),
        P(),
    )
    return jax.shard_map(
        local, mesh=mesh, in_specs=placed, out_specs=P("lat", "lon", None), check_vma=False
    )
```

profile of v0, /device:TPU:1, one launch (start us, length us, event | category | flops | bytes accessed | tf_op | source)
XLA Modules:
  0.0 1329.8 jit_solution(5070489163931986096)
XLA Ops:
  6.5 0.0 copy-start
  6.5 0.0 all-gather.4.cloned.1.call-start
  6.5 1.5 fusion.79
  8.0 4.0 collective-permute-start
  12.0 13.0 collective-permute-start.1
  25.1 1.1 fusion.80
  26.3 1.2 fusion.81
  27.5 1.1 constant_dynamic-update-slice_fusion.1
  28.6 1.1 fusion.82
  29.7 0.0 collective-permute-done
  29.7 0.4 collective-permute-done.1
  30.1 0.0 copy-done
  30.1 0.1 pad_maximum_fusion.4
  30.2 6.0 collective-permute-start.2
  36.1 0.0 copy-start.1
  36.1 1.9 collective-permute-start.3
  38.1 0.2 constant_dynamic-update-slice_fusion
  38.3 0.0 collective-permute-done.2
  38.3 5.3 collective-permute-done.3
  43.6 0.7 maximum_maximum_fusion
  44.2 0.0 copy-done.1
  44.3 0.0 copy-start.2
  44.3 0.0 copy-start.3
  44.3 9.4 fusion.77
  53.7 0.0 copy-start.6
  53.7 0.3 multiply_reduce_fusion
  54.0 0.0 copy-done.2
  54.0 0.0 copy-done.3
  54.0 1.0 fusion.44
  55.1 0.0 all-gather.4.cloned.1.call-update
  55.1 0.0 all-gather.6.cloned.1.call-start
  55.1 0.7 all-gather.6.cloned.1.call-update
  55.8 0.0 all-gather.8.cloned.1.call-start
  55.9 0.7 all-gather.8.cloned.1.call-update
  56.6 0.0 reduce-scatter.2.cloned.1.call-start
  56.6 30.5 %all-gather.4.cloned.1.call-done = bf16[1024,1024]{1,0:T(8,128)(2,1)} async-done(((bf16[256,1024]{1,0:T(8,128)(2,1)}), bf16[1024,1024]{1,0:T(8,128)(2,1)}) %all-gather.4.cloned.1.call-update) | async-done | bytes 2097168 | tf_op jit(solution)/shard_map/all_gather | solution.py:51
  87.2 503.7 %all-gather.6.cloned.1.call-done = bf16[1024,1024]{1,0:T(8,128)(2,1)} async-done(((bf16[8,1024]{1,0:T(8,128)(2,1)}), bf16[1024,1024]{1,0:T(8,128)(2,1)}) %all-gather.6.cloned.1.call-update) | async-done | bytes 2097168 | tf_op jit(solution)/shard_map/all_gather | solution.py:55
  590.9 582.4 %all-gather.8.cloned.1.call-done = bf16[1024,1024]{1,0:T(8,128)(2,1)} async-done(((bf16[8,1024]{1,0:T(8,128)(2,1)}), bf16[1024,1024]{1,0:T(8,128)(2,1)}) %all-gather.8.cloned.1.call-update) | async-done | bytes 2097168 | tf_op jit(solution)/shard_map/all_gather | solution.py:63
  1173.3 0.0 copy-done.6
  1173.3 16.1 %fusion.14 = bf16[1024,1024]{1,0:T(8,128)(2,1)} fusion(bf16[1024,1024]{1,0:T(8,128)(2,1)} %all-gather.8.cloned.1.call-done, f32[1024]{0:T(1024)S(1)} %copy-done.6, bf16[1024,1024]{1,0:T(8,128)(2,1)} %all-gather.4.cloned.1.call-done, bf16[1024,1024]{1,0:T(8,128)(2,1)} %all-gather.6.cloned.1.call-done), kind=kOutput, calls=%fused_computation.21 | convolution fusion | flops 4365221888 | bytes 8392704 | tf_op jit(solution)/shard_map/dot_general | solution.py:61
  1189.4 0.0 copy-start.4
  1189.4 0.0 copy-start.5
  1189.4 0.0 reduce-scatter.2.cloned.1.call-update
  1189.5 131.8 %reduce-scatter.2.cloned.1.call-done = bf16[256,1024]{1,0:T(8,128)(2,1)} async-done(((bf16[1024,1024]{1,0:T(8,128)(2,1)}), bf16[256,1024]{1,0:T(8,128)(2,1)}) %reduce-scatter.2.cloned.1.call-update) | async-done | bytes 524304 | tf_op jit(solution)/shard_map/reduce_scatter | solution.py:67
  1321.2 0.0 copy-done.4
  1321.2 0.0 copy-done.5
  1321.2 2.0 fusion.42
  (2 shorter events, 0.0 us)
Async XLA Ops:
  6.5 23.5 %copy-start = (bf16[32,8,1024]{2,1,0:T(8,128)(2,1)S(1)}, bf16[32,8,1024]{2,1,0:T(8,128)(2,1)}, u32[]{:S(2)}) copy-start(bf16[32,8,1024]{2,1,0:T(8,128)(2,1)} %param.10) | copy-start | bytes 1572868
  6.5 80.6 %all-gather.4.cloned.1.call-start = ((), (), s32[]{:S(2)}) async-start(), calls=%async_computation.1 | async-start | bytes 2621440 | tf_op jit(solution)/shard_map/all_gather | solution.py:51
  8.0 21.7 %collective-permute-start = (bf16[32,3,1024]{2,1,0:T(4,128)(2,1)S(1)}, bf16[32,3,1024]{2,1,0:T(4,128)(2,1)S(1)}, u32[]{:S(2)}, u32[]{:S(2)}) collective-permute-start(bf16[32,3,1024]{2,1,0:T(4,128)(2,1)S(1)} %get-tuple-element.11), channel_id=1, source_target_pairs={{0,1},{1,2},{2,3},{3,4},{4,5},{5,6},{6,7},{7,8},{8,9},{9,10},{10,1... | collective-permute-start | bytes 589832 | tf_op jit(solution)/shard_map/ppermute | solution.py:14
  12.0 18.0 %collective-permute-start.1 = (bf16[32,3,1024]{2,1,0:T(4,128)(2,1)S(1)}, bf16[32,3,1024]{2,1,0:T(4,128)(2,1)S(1)}, u32[]{:S(2)}, u32[]{:S(2)}) collective-permute-start(bf16[32,3,1024]{2,1,0:T(4,128)(2,1)S(1)} %get-tuple-element.12), channel_id=1, source_target_pairs={{1,0},{2,1},{3,2},{4,3},{5,4},{6,5},{7,6},{8,7},{9,8},{10,9},{11,1... | collective-permute-start | bytes 589832 | tf_op jit(solution)/shard_map/ppermute | solution.py:17
  30.2 8.1 collective-permute-start.2
  36.1 8.1 copy-start.1
  36.1 7.4 collective-permute-start.3
  44.3 9.7 copy-start.2
  44.3 9.7 copy-start.3
  53.7 1119.6 %copy-start.6 = (f32[1024]{0:T(1024)S(1)}, f32[1024]{0:T(1024)}, u32[]{:S(2)}) copy-start(f32[1024]{0:T(1024)} %param.16) | copy-start | bytes 12292
  55.1 535.8 %all-gather.6.cloned.1.call-start = ((), (), s32[]{:S(2)}) async-start(), calls=%async_computation.2 | async-start | bytes 2113536 | tf_op jit(solution)/shard_map/all_gather | solution.py:55
  55.8 1117.5 %all-gather.8.cloned.1.call-start = ((), (), s32[]{:S(2)}) async-start(), calls=%async_computation.3 | async-start | bytes 2113536 | tf_op jit(solution)/shard_map/all_gather | solution.py:63
  56.6 1264.7 %reduce-scatter.2.cloned.1.call-start = ((), (), s32[]{:S(2)}) async-start(), calls=%async_computation.4 | async-start | bytes 2621440 | tf_op jit(solution)/shard_map/reduce_scatter | solution.py:67
  1189.4 131.8 %copy-start.4 = (f32[1024]{0:T(1024)S(1)}, f32[1024]{0:T(1024)}, u32[]{:S(2)}) copy-start(f32[1024]{0:T(1024)} %param.18) | copy-start | bytes 12292
  1189.4 131.8 %copy-start.5 = (f32[1024]{0:T(1024)S(1)}, f32[1024]{0:T(1024)}, u32[]{:S(2)}) copy-start(f32[1024]{0:T(1024)} %param.19) | copy-start | bytes 12292
Sparse Core Ops, SparseCore 0:
  55.2 31.9 all-gather.3
  89.2 501.5 all-gather.5
  592.9 580.2 all-gather.7
  1189.6 131.5 reduce-scatter.1
where the time goes:
time: 1330 us
  waiting for transfers between devices  1260 us (95%)
  starting transfers between devices  25.1 us (2%)
  matrix products  16.1 us (1%)
  other arithmetic  13.5 us (1%)
  between operations  13.3 us (1%)
    all_gather x1, waiting for transfers between devices, local(): lax.all_gather(down_weight, 'lon', axis=0, tiled=True)  582 us
    all_gather x1, waiting for transfers between devices, local(): lax.all_gather(up_weight, 'lon', axis=0, tiled=True)  504 us
    reduce_scatter x1, waiting for transfers between devices, local(): lax.psum_scatter(partial_out.astype(jnp.bfloat16), 'lat', scatter_dimensi...  132 us
    all_gather x1, waiting for transfers between devices, local(): gathered = lax.all_gather(normed, 'lat', axis=0, tiled=True)  30.5 us
  transfers between devices with their start and end apart: 8, of which 6 were waited for; matrix products, arithmetic and copies ran while one was open for 0% of the time, Pallas kernels for 0%

commit v1 on v0

--- a/solution.py
+++ b/solution.py
@@ -17,6 +17,21 @@
         high = lax.ppermute(lax.slice_in_dim(block, 0, width, axis=dim), axis, backward)
         block = jnp.concatenate([low, block, high], axis=dim)
     return block
+
+
+def staged_gather(shard):
+    count = lax.axis_size("lon")
+    n_x, n_y = 4, 2
+    n_z = count // (n_x * n_y)
+    index = lambda x, z, y: (x * n_z + z) * n_y + y
+    by_y = [[index(x, z, y) for y in range(n_y)] for x in range(n_x) for z in range(n_z)]
+    by_x = [[index(x, z, y) for x in range(n_x)] for z in range(n_z) for y in range(n_y)]
+    by_z = [[index(x, z, y) for z in range(n_z)] for x in range(n_x) for y in range(n_y)]
+    part = lax.all_gather(shard, "lon", axis=0, axis_index_groups=by_y)
+    part = lax.all_gather(part, "lon", axis=0, axis_index_groups=by_x)
+    part = lax.all_gather(part, "lon", axis=0, axis_index_groups=by_z)
+    part = jnp.swapaxes(part, 0, 1)
+    return part.reshape((count * shard.shape[0],) + shard.shape[1:])
 
 
 def local(
@@ -52,7 +67,7 @@
     pre = (
         jnp.dot(
             gathered,
-            lax.all_gather(up_weight, "lon", axis=0, tiled=True),
+            staged_gather(up_weight),
             preferred_element_type=jnp.float32,
         )
         + up_bias
@@ -60,7 +75,7 @@
     hidden = jax.nn.gelu(pre, approximate=False).astype(jnp.bfloat16)
     partial_out = lax.dot_general(
         hidden,
-        lax.all_gather(down_weight, "lon", axis=0, tiled=True),
+        staged_gather(down_weight),
         (((1,), (1,)), ((), ())),
         preferred_element_type=jnp.float32,
     )

time: 1330 us -> 286 us (0.22)
  waiting for transfers between devices: 1260 us -> 176 us
  blocking collectives: 0 us -> 28.5 us
    all_gather x2, waiting for transfers between devices: 1090 us -> 77.6 us  [staged_gather(): part = lax.all_gather(part, 'lon', axis=0, axis_index_groups=by_z)]
    reduce_scatter x1, waiting for transfers between devices: 132 us -> 53 us  [local(): lax.psum_scatter(partial_out.astype(jnp.bfloat16), 'lat', scatter_dimensi...]
    all_gather x0 -> x4, blocking collectives: none -> 28.5 us  [the longest x2 20.1 us: staged_gather(): part = lax.all_gather(part, 'lon', axis=0, axis_index_groups=by_x)]
  transfers between devices with their start and end apart: 8 -> 8, of which waited for: 6 -> 5; matrix products, arithmetic and copies ran while one was open for 0% -> 7% of each run, Pallas kernels for 0% -> 0%
where the time goes in v1:
time: 286 us
  waiting for transfers between devices  176 us (62%)
  starting transfers between devices  31 us (11%)
  blocking collectives  28.5 us (10%)
  matrix products  15.5 us (5%)
  other arithmetic  13.5 us (5%)
  between operations  13.3 us (5%)
  local copies, waits for them, and re-layouts  7.98 us (3%)
    all_gather x2, waiting for transfers between devices, staged_gather(): part = lax.all_gather(part, 'lon', axis=0, axis_index_groups=by_z)  77.6 us
    reduce_scatter x1, waiting for transfers between devices, local(): lax.psum_scatter(partial_out.astype(jnp.bfloat16), 'lat', scatter_dimensi...  53 us
    all_gather x1, waiting for transfers between devices, local(): gathered = lax.all_gather(normed, 'lat', axis=0, tiled=True)  39.6 us
    all_gather x2, blocking collectives, staged_gather(): part = lax.all_gather(part, 'lon', axis=0, axis_index_groups=by_x)  20.1 us
    ppermute x2, starting transfers between devices, with_halo(): lax.ppermute(lax.slice_in_dim(block, block.shape[dim] - width, None, axis...  16.1 us
    dot_general x1, matrix products, local(): lax.dot_general(hidden, staged_gather(down_weight), (((1,), (1,)), ((), (...  15.5 us
    ppermute x2, starting transfers between devices, with_halo(): lax.ppermute(lax.slice_in_dim(block, 0, width, axis=dim), axis, backward)  14.6 us
    reduce_sum x1, other arithmetic, local(): centre = jnp.mean(total, axis=-1, keepdims=True)  9.42 us
  transfers between devices with their start and end apart: 8, of which 5 were waited for; matrix products, arithmetic and copies ran while one was open for 7% of the time, Pallas kernels for 0%

profile of v1, /device:TPU:1, one launch (start us, length us, event | category | flops | bytes accessed | tf_op | source)
XLA Modules:
  0.0 285.6 jit_solution(13402974047549205243)
XLA Ops:
  6.5 0.0 copy-start
  6.5 0.0 copy-start.1
  6.5 0.0 all-gather.12.cloned.1.call-start
  6.5 4.3 %all-gather = bf16[16,1024]{1,0:T(8,128)(2,1)S(1)} all-gather(bf16[8,1024]{1,0:T(8,128)(2,1)} %param.15), channel_id=2, replica_groups={{0,1},{2,3},{4,5},{6,7},{8,9},{10,11},{12,13},{14,15},{16,17},{18,19},{..., dimensions={0}, use_global_device_ids=true | all-gather | bytes 49152 | tf_op jit(solution)/shard_map/all_gather | solution.py:30
  10.8 10.3 %all-gather.1 = bf16[8,8,1024]{2,1,0:T(8,128)(2,1)} all-gather(bf16[2,8,1024]{2,1,0:T(8,128)(2,1)S(1)} %bitcast.75), channel_id=3, replica_groups={{0,32,64,96},{1,33,65,97},{2,34,66,98},{3,35,67,99},{4,36,68,100},{5,37..., dimensions={0}, use_global_device_ids=true | all-gather | bytes 163840 | tf_op jit(solution)/shard_map/all_gather | solution.py:31
  21.1 0.0 all-gather.12.cloned.1.call-update
  21.2 0.0 all-gather.14.cloned.1.call-start
  21.2 1.4 fusion.79
  22.7 3.2 %collective-permute-start = (bf16[32,3,1024]{2,1,0:T(4,128)(2,1)S(1)}, bf16[32,3,1024]{2,1,0:T(4,128)(2,1)S(1)}, u32[]{:S(2)}, u32[]{:S(2)}) collective-permute-start(bf16[32,3,1024]{2,1,0:T(4,128)(2,1)S(1)} %get-tuple-element.11), channel_id=1, source_target_pairs={{0,1},{1,2},{2,3},{3,4},{4,5},{5,6},{6,7},{7,8},{8,9},{9,10},{10,1... | collective-permute-start | bytes 589832 | tf_op jit(solution)/shard_map/ppermute | solution.py:14
  25.9 12.7 %collective-permute-start.1 = (bf16[32,3,1024]{2,1,0:T(4,128)(2,1)S(1)}, bf16[32,3,1024]{2,1,0:T(4,128)(2,1)S(1)}, u32[]{:S(2)}, u32[]{:S(2)}) collective-permute-start(bf16[32,3,1024]{2,1,0:T(4,128)(2,1)S(1)} %get-tuple-element.12), channel_id=1, source_target_pairs={{1,0},{2,1},{3,2},{4,3},{5,4},{6,5},{7,6},{8,7},{9,8},{10,9},{11,1... | collective-permute-start | bytes 589832 | tf_op jit(solution)/shard_map/ppermute | solution.py:17
  38.6 4.0 %all-gather.3 = bf16[16,1024]{1,0:T(8,128)(2,1)S(1)} all-gather(bf16[8,1024]{1,0:T(8,128)(2,1)} %param.17), channel_id=5, replica_groups={{0,1},{2,3},{4,5},{6,7},{8,9},{10,11},{12,13},{14,15},{16,17},{18,19},{..., dimensions={0}, use_global_device_ids=true | all-gather | bytes 49152 | tf_op jit(solution)/shard_map/all_gather | solution.py:30
  42.6 9.8 %all-gather.4 = bf16[8,8,1024]{2,1,0:T(8,128)(2,1)} all-gather(bf16[2,8,1024]{2,1,0:T(8,128)(2,1)S(1)} %bitcast.76), channel_id=6, replica_groups={{0,32,64,96},{1,33,65,97},{2,34,66,98},{3,35,67,99},{4,36,68,100},{5,37..., dimensions={0}, use_global_device_ids=true | all-gather | bytes 163840 | tf_op jit(solution)/shard_map/all_gather | solution.py:31
  52.5 0.0 all-gather.14.cloned.1.call-update
  52.5 0.0 all-gather.10.cloned.1.call-start
  52.5 1.2 fusion.80
  53.7 0.0 copy-done
  53.7 0.0 copy-done.1
  53.8 0.1 fusion.81
  53.9 0.0 collective-permute-done
  53.9 0.0 collective-permute-done.1
  53.9 0.1 pad_maximum_fusion.4
  54.0 12.9 %collective-permute-start.2 = (bf16[3,14,1024]{2,1,0:T(8,128)(2,1)S(1)}, bf16[3,14,1024]{2,1,0:T(8,128)(2,1)S(1)}, u32[]{:S(2)}, u32[]{:S(2)}) collective-permute-start(bf16[3,14,1024]{2,1,0:T(8,128)(2,1)S(1)} %get-tuple-element.9), channel_id=1, source_target_pairs={{0,128},{128,256},{256,384},{1,129},{129,257},{257,385},{2,130},{1... | collective-permute-start | bytes 258056 | tf_op jit(solution)/shard_map/ppermute | solution.py:14
  66.9 0.0 copy-start.2
  66.9 1.9 collective-permute-start.3
  68.8 0.2 constant_dynamic-update-slice_fusion
  69.0 0.0 collective-permute-done.2
  69.0 5.4 %collective-permute-done.3 = bf16[3,14,1024]{2,1,0:T(8,128)(2,1)S(1)} collective-permute-done((bf16[3,14,1024]{2,1,0:T(8,128)(2,1)S(1)}, bf16[3,14,1024]{2,1,0:T(8,128)(2,1)S(1)}, u32[]{:S(2)}, u32[]{:S(2)}) %collective-permute-start.3) | collective-permute-done | bytes 86048 | tf_op jit(solution)/shard_map/ppermute | solution.py:17
  74.4 0.6 maximum_maximum_fusion
  75.0 0.0 copy-done.2
  75.0 0.0 copy-start.3
  75.1 0.0 copy-start.4
  75.1 9.4 %fusion.77 = (f32[32,8]{1,0:T(8,128)S(1)}, f32[32,8,1024]{2,1,0:T(8,128)S(1)}) fusion(f32[1024]{0:T(1024)S(1)} %bitcast.125, bf16[35,14,1024]{2,1,0:T(8,128)(2,1)S(1)} %get-tuple-element.8, f32[1024]{0:T(1024)S(1)} %bitcast.124, f32[1024]{0:T(1024)S(1)} %bitcast.123, f32[1024]{0:T(1024)S(1)} %bitcast.122, f32[1024]{0:T(1024)S(1)} %bitcast.121, ...), kind=kLoop, calls=%fused_computation.101 | loop fusion | flops 41156352 | bytes 25568256 | tf_op jit(solution)/shard_map/reduce_sum | solution.py:60
  84.5 0.3 multiply_reduce_fusion
  84.8 0.0 copy-done.3
  84.8 0.0 copy-done.4
  84.8 1.0 fusion.44
  85.8 0.0 all-gather.10.cloned.1.call-update
  85.9 0.2 reduce-scatter.2.cloned.1.call-start
  86.1 7.4 %all-gather.12.cloned.1.call-done = bf16[64,2,8,1024]{3,2,1,0:T(8,128)(2,1)} async-done(((bf16[4,2,8,1024]{3,2,1,0:T(8,128)(2,1)}), bf16[64,2,8,1024]{3,2,1,0:T(8,128)(2,1)}) %all-gather.12.cloned.1.call-update) | async-done | bytes 2097168 | tf_op jit(solution)/shard_map/all_gather | solution.py:32
  93.5 1.8 copy.13
  95.3 70.2 %all-gather.14.cloned.1.call-done = bf16[64,2,8,1024]{3,2,1,0:T(8,128)(2,1)} async-done(((bf16[4,2,8,1024]{3,2,1,0:T(8,128)(2,1)}), bf16[64,2,8,1024]{3,2,1,0:T(8,128)(2,1)}) %all-gather.14.cloned.1.call-update) | async-done | bytes 2097168 | tf_op jit(solution)/shard_map/all_gather | solution.py:32
  165.5 0.0 copy-start.7
  165.5 3.3 %copy.14 = bf16[4,16,2,8,1024]{4,3,2,1,0:T(8,128)(2,1)} copy(bf16[4,16,2,8,1024]{4,3,2,0,1:T(8,128)(2,1)} %bitcast.70) | data formatting | bytes 4194304 | tf_op jit(solution)/shard_map/transpose | solution.py:33
  168.8 39.6 %all-gather.10.cloned.1.call-done = bf16[1024,1024]{1,0:T(8,128)(2,1)} async-done(((bf16[256,1024]{1,0:T(8,128)(2,1)}), bf16[1024,1024]{1,0:T(8,128)(2,1)}) %all-gather.10.cloned.1.call-update) | async-done | bytes 2097168 | tf_op jit(solution)/shard_map/all_gather | solution.py:66
  208.4 0.0 copy-done.7
  208.4 15.5 %fusion.14 = bf16[1024,1024]{1,0:T(8,128)(2,1)} fusion(bf16[1024,1024]{1,0:T(8,128)(2,1)} %bitcast.72, f32[1024]{0:T(1024)S(1)} %copy-done.7, bf16[1024,1024]{1,0:T(8,128)(2,1)} %all-gather.10.cloned.1.call-done, bf16[1024,1024]{1,0:T(8,128)(2,1)S(1)} %bitcast.71), kind=kOutput, calls=%fused_computation.21 | convolution fusion | flops 4365221888 | bytes 8392704 | tf_op jit(solution)/shard_map/dot_general | solution.py:76
  223.9 0.0 copy-start.5
  223.9 0.0 copy-start.6
  223.9 0.0 reduce-scatter.2.cloned.1.call-update
  224.0 53.0 %reduce-scatter.2.cloned.1.call-done = bf16[256,1024]{1,0:T(8,128)(2,1)} async-done(((bf16[1024,1024]{1,0:T(8,128)(2,1)}), bf16[256,1024]{1,0:T(8,128)(2,1)}) %reduce-scatter.2.cloned.1.call-update) | async-done | bytes 524304 | tf_op jit(solution)/shard_map/reduce_scatter | solution.py:82
  277.0 0.0 copy-done.5
  277.0 0.0 copy-done.6
  277.0 2.0 fusion.42
  (4 shorter events, 0.1 us)
Async XLA Ops:
  6.5 47.2 %copy-start = (bf16[32,8,1024]{2,1,0:T(8,128)(2,1)S(1)}, bf16[32,8,1024]{2,1,0:T(8,128)(2,1)}, u32[]{:S(2)}) copy-start(bf16[32,8,1024]{2,1,0:T(8,128)(2,1)} %param.10) | copy-start | bytes 1572868
  6.5 47.2 %copy-start.1 = (bf16[7,7,1024]{2,1,0:T(8,128)(2,1)S(1)}, bf16[7,7,1024]{2,1,0:T(8,128)(2,1)}, u32[]{:S(2)}) copy-start(bf16[7,7,1024]{2,1,0:T(8,128)(2,1)} %param.11) | copy-start | bytes 301060
  6.5 87.0 %all-gather.12.cloned.1.call-start = ((), (), s32[]{:S(2)}) async-start(), calls=%async_computation.3 | async-start | bytes 2228224 | tf_op jit(solution)/shard_map/all_gather | solution.py:32
  21.2 144.3 %all-gather.14.cloned.1.call-start = ((), (), s32[]{:S(2)}) async-start(), calls=%async_computation.4 | async-start | bytes 2228224 | tf_op jit(solution)/shard_map/all_gather | solution.py:32
  22.7 31.2 %collective-permute-start = (bf16[32,3,1024]{2,1,0:T(4,128)(2,1)S(1)}, bf16[32,3,1024]{2,1,0:T(4,128)(2,1)S(1)}, u32[]{:S(2)}, u32[]{:S(2)}) collective-permute-start(bf16[32,3,1024]{2,1,0:T(4,128)(2,1)S(1)} %get-tuple-element.11), channel_id=1, source_target_pairs={{0,1},{1,2},{2,3},{3,4},{4,5},{5,6},{6,7},{7,8},{8,9},{9,10},{10,1... | collective-permute-start | bytes 589832 | tf_op jit(solution)/shard_map/ppermute | solution.py:14
  25.9 28.0 %collective-permute-start.1 = (bf16[32,3,1024]{2,1,0:T(4,128)(2,1)S(1)}, bf16[32,3,1024]{2,1,0:T(4,128)(2,1)S(1)}, u32[]{:S(2)}, u32[]{:S(2)}) collective-permute-start(bf16[32,3,1024]{2,1,0:T(4,128)(2,1)S(1)} %get-tuple-element.12), channel_id=1, source_target_pairs={{1,0},{2,1},{3,2},{4,3},{5,4},{6,5},{7,6},{8,7},{9,8},{10,9},{11,1... | collective-permute-start | bytes 589832 | tf_op jit(solution)/shard_map/ppermute | solution.py:17
  52.5 155.9 %all-gather.10.cloned.1.call-start = ((), (), s32[]{:S(2)}) async-start(), calls=%async_computation.1 | async-start | bytes 2621440 | tf_op jit(solution)/shard_map/all_gather | solution.py:66
  54.0 15.0 %collective-permute-start.2 = (bf16[3,14,1024]{2,1,0:T(8,128)(2,1)S(1)}, bf16[3,14,1024]{2,1,0:T(8,128)(2,1)S(1)}, u32[]{:S(2)}, u32[]{:S(2)}) collective-permute-start(bf16[3,14,1024]{2,1,0:T(8,128)(2,1)S(1)} %get-tuple-element.9), channel_id=1, source_target_pairs={{0,128},{128,256},{256,384},{1,129},{129,257},{257,385},{2,130},{1... | collective-permute-start | bytes 258056 | tf_op jit(solution)/shard_map/ppermute | solution.py:14
  66.9 8.2 %copy-start.2 = (f32[1024]{0:T(1024)S(1)}, f32[1024]{0:T(1024)}, u32[]{:S(2)}) copy-start(f32[1024]{0:T(1024)} %param.12) | copy-start | bytes 12292
  66.9 7.5 %collective-permute-start.3 = (bf16[3,14,1024]{2,1,0:T(8,128)(2,1)S(1)}, bf16[3,14,1024]{2,1,0:T(8,128)(2,1)S(1)}, u32[]{:S(2)}, u32[]{:S(2)}) collective-permute-start(bf16[3,14,1024]{2,1,0:T(8,128)(2,1)S(1)} %get-tuple-element.10), channel_id=1, source_target_pairs={{128,0},{256,128},{384,256},{129,1},{257,129},{385,257},{130,2},{2... | collective-permute-start | bytes 258056 | tf_op jit(solution)/shard_map/ppermute | solution.py:17
  75.0 9.7 %copy-start.3 = (f32[1024]{0:T(1024)S(1)}, f32[1024]{0:T(1024)}, u32[]{:S(2)}) copy-start(f32[1024]{0:T(1024)} %param.14) | copy-start | bytes 12292
  75.1 9.7 %copy-start.4 = (f32[1024]{0:T(1024)S(1)}, f32[1024]{0:T(1024)}, u32[]{:S(2)}) copy-start(f32[1024]{0:T(1024)} %param.13) | copy-start | bytes 12292
  85.9 191.1 %reduce-scatter.2.cloned.1.call-start = ((), (), s32[]{:S(2)}) async-start(), calls=%async_computation.2 | async-start | bytes 2621440 | tf_op jit(solution)/shard_map/reduce_scatter | solution.py:82
  165.5 42.9 %copy-start.7 = (f32[1024]{0:T(1024)S(1)}, f32[1024]{0:T(1024)}, u32[]{:S(2)}) copy-start(f32[1024]{0:T(1024)} %param.16) | copy-start | bytes 12292
  223.9 53.1 %copy-start.5 = (f32[1024]{0:T(1024)S(1)}, f32[1024]{0:T(1024)}, u32[]{:S(2)}) copy-start(f32[1024]{0:T(1024)} %param.18) | copy-start | bytes 12292
  223.9 53.1 %copy-start.6 = (f32[1024]{0:T(1024)S(1)}, f32[1024]{0:T(1024)}, u32[]{:S(2)}) copy-start(f32[1024]{0:T(1024)} %param.19) | copy-start | bytes 12292
Sparse Core Ops, SparseCore 0:
  21.3 72.1 all-gather.11
  95.6 69.8 all-gather.13
  167.6 40.7 all-gather.9
  224.1 52.8 reduce-scatter.1

commit v2 on v0

v2 whole, which is shorter than its diff:
```python
import functools

import jax
import jax.numpy as jnp
from jax import lax
from jax.experimental import pallas as pl
from jax.experimental.pallas import tpu as pltpu
from jax.sharding import PartitionSpec as P

MESH = pl.DeviceIdType.MESH
NX, NZ, NY = 4, 16, 2
STEPS = NZ // 2


def remote(src, dst, send_sem, recv_sem, device):
    return pltpu.make_async_remote_copy(
        src_ref=src, dst_ref=dst, send_sem=send_sem, recv_sem=recv_sem, device_id=device, device_id_type=MESH
    )


def kernel(
    feat, dker, dbias, gain, nbias, up, ubias, down, obias, scale,
    out,
    wts, ybuf, xpad, kers, conv, csend, crecv, rrecv, acts, hid, own, s_sib, s_mid, s_crs, r_sib, r_mid, r_crs,
    y_ss, y_rs, h_ss, h_rs, x1_ss, x1_rs, x2_ss, x2_rs, z1_ss, z1_rs, z2_ss, z2_rs, a_ss, a_rs, o_ss, o_rs,
):
    f32, bf16 = jnp.float32, jnp.bfloat16
    rows, cols, chans = feat.shape
    hidden = up.shape[1]
    tiles = chans // 128
    half = hidden // 2
    blocks = rows // 8
    chunk = 8 * cols
    pixels = rows * cols
    n_lon = NX * NZ * NY
    lat = lax.axis_index("lat")
    lon = lax.axis_index("lon")
    y = lax.rem(lon, NY)
    z = lax.rem(lon // NY, NZ)
    x = lon // (NY * NZ)

    def at(x_, z_):
        return (lat, (lax.rem(x_ + NX, NX) * NZ + lax.rem(z_ + NZ, NZ)) * NY + y)

    flip = lat + 1 - 2 * lax.rem(lat, 2)
    far = lax.rem(lat + 2, 4)
    far_flip = lax.rem(flip + 2, 4)
    pair_lon = lon + 1 - 2 * y
    pair = (lat, pair_lon)
    sib = (flip, lon)
    crs = (far, pair_lon)
    east = lax.rem(lon + 1, n_lon)
    west = lax.rem(lon + n_lon - 1, n_lon)
    has_up = lat > 0
    has_down = lat < 3

    barrier = pltpu.get_barrier_semaphore()

    def hello(device):
        pl.semaphore_signal(barrier, inc=1, device_id=device, device_id_type=MESH)

    near = [pair, sib, crs, (lat, east), (lat, west), at(x, z + 1), at(x, z - 1)]
    near += [at(x + k, z) for k in range(1, NX)]
    for device in near:
        hello(device)

    @pl.when(has_up)
    def _():
        for lon_ in (west, lon, east):
            hello((lat - 1, lon_))

    @pl.when(has_down)
    def _():
        for lon_ in (west, lon, east):
            hello((lat + 1, lon_))

    for a in range(7):
        kers[a, 0:7, :] = dker[a].astype(f32)

    low4 = lax.broadcasted_iota(jnp.int32, (8, chans), 0) < 4

    def pack(q, _):
        v = [feat[4 * q + i].astype(f32) for i in range(4)]
        turned = [pltpu.roll(t, 4, 0) for t in v]
        right = [jnp.where(low4, turned[i], v[i + 1]) for i in (0, 2)]
        left = [jnp.where(low4, v[i], turned[i + 1]) for i in (0, 2)]
        csend[0, q] = jnp.concatenate(right, 0).astype(bf16)
        csend[1, q] = jnp.concatenate(left, 0).astype(bf16)
        return 0

    lax.fori_loop(0, rows // 4, pack, 0)
    pl.semaphore_wait(barrier, len(near) + 3 * has_up.astype(jnp.int32) + 3 * has_down.astype(jnp.int32))

    ycopy = [remote((up, down)[w], ybuf.at[w], y_ss.at[w], y_rs.at[w], pair) for w in range(2)]
    for c in ycopy:
        c.start()

    last = rows // 4 - 1
    to_east = remote(csend.at[0], crecv.at[0, pl.ds(1, last + 1)], h_ss.at[0], h_rs.at[0], (lat, east))
    to_west = remote(csend.at[1], crecv.at[1, pl.ds(1, last + 1)], h_ss.at[1], h_rs.at[1], (lat, west))
    to_east.start()
    to_west.start()
    to_down = [
        remote(feat.at[pl.ds(rows - 3, 3)], rrecv.at[0], h_ss.at[2], h_rs.at[2], (lat + 1, lon)),
        remote(csend.at[0, last], crecv.at[0, 0], h_ss.at[3], h_rs.at[3], (lat + 1, east)),
        remote(csend.at[1, last], crecv.at[1, 0], h_ss.at[4], h_rs.at[4], (lat + 1, west)),
    ]
    to_up = [
        remote(feat.at[pl.ds(0, 3)], rrecv.at[1], h_ss.at[5], h_rs.at[5], (lat - 1, lon)),
        remote(csend.at[0, 0], crecv.at[0, last + 2], h_ss.at[6], h_rs.at[6], (lat - 1, east)),
        remote(csend.at[1, 0], crecv.at[1, last + 2], h_ss.at[7], h_rs.at[7], (lat - 1, west)),
    ]

    @pl.when(has_down)
    def _():
        for c in to_down:
            c.start()

    @pl.when(has_up)
    def _():
        for c in to_up:
            c.start()

    def widen(h, _):
        v = feat[h].astype(f32)
        for t in range(tiles):
            xpad[t, h + 4, 8:16, :] = v[:, t * 128 : (t + 1) * 128]
        return 0

    lax.fori_loop(0, rows, widen, 0)

    prow = 2 * up.shape[0]

    def wide(w, zb):
        return wts.at[w, :, pl.ds(pl.multiple_of(zb * prow, prow), prow), pl.ds(0, half)]

    def thin(w, xb, zb):
        return wts.at[w, xb, pl.ds(pl.multiple_of(zb * prow, prow), prow), pl.ds(half, half)]

    def first(w, xb, zb):
        return wts.at[w, xb, pl.ds(pl.multiple_of(zb * prow, prow), prow), pl.ds(0, half)]

    def length(w, d):
        return STEPS if w == d else STEPS - 1

    def block(d, s):
        return lax.rem(z + (NZ - s if d == 0 else s), NZ)

    def z1(w, d, s):
        ref = wide(w, block(d, s))
        return remote(ref, ref, z1_ss.at[w, d, s], z1_rs.at[w, d, s], at(x, z + 1 if d == 0 else z - 1))

    def z2(w, d, s):
        ref = thin(w, x, block(d, s))
        return remote(ref, ref, z2_ss.at[w, d, s], z2_rs.at[w, d, s], at(x, z + 1 if d == 0 else z - 1))

    def x1(w, k):
        ref = first(w, x, z)
        return remote(ref, ref, x1_ss.at[w, k - 1], x1_rs.at[w, k - 1], at(x + k, z))

    def x2(w, k, zb):
        ref = thin(w, x, zb)
        return remote(ref, ref, x2_ss.at[w, k - 1], x2_rs.at[w, k - 1], at(x + k, z))

    for w in range(2):
        ycopy[w].wait_recv()
        mine = (up, down)[w][...].astype(f32)
        other = ybuf[w].astype(f32)
        is_low = y == 0
        both = jnp.concatenate([jnp.where(is_low, mine, other), jnp.where(is_low, other, mine)], 0)
        wts[w, x, pl.ds(pl.multiple_of(z * prow, prow), prow), :] = both.astype(bf16)
        for k in range(1, NX):
            x1(w, k).start()
        for d in range(2):
            z2(w, d, 0).start()
        for k in range(1, NX):
            x2(w, k, z).start()

    def serve(w, s, final=False):
        for d in range(2):
            z2(w, d, s).wait_recv()
            if not final:
                z2(w, d, s + 1).start()
            for k in range(1, NX):
                x2(w, k, block(d, s + 1)).start()
        for d in range(2):
            z1(w, d, s).wait_recv()
            if not final:
                z1(w, d, s + 1).start()

    def serve_end(w):
        s = STEPS - 2
        long, short = w, 1 - w
        z2(w, long, s).wait_recv()
        z2(w, long, s + 1).start()
        for k in range(1, NX):
            x2(w, k, block(long, s + 1)).start()
        z1(w, long, s).wait_recv()
        z1(w, long, s + 1).start()
        z2(w, short, s).wait_recv()
        for k in range(1, NX):
            x2(w, k, block(short, s + 1)).start()
        z1(w, short, s).wait_recv()

    def serve_last(w):
        s = STEPS - 1
        z2(w, w, s).wait_recv()
        for k in range(1, NX):
            x2(w, k, block(w, s + 1)).start()
        z1(w, w, s).wait_recv()

    def whole(w, k):
        ref = wts.at[w, 0, :, pl.ds(0, half)]
        return remote(ref, ref, x2_ss.at[w, k - 1], x2_rs.at[w, k - 1], at(x + k, z))

    for w in range(2):
        for k in range(1, NX):
            x1(w, k).wait_recv()
        for d in range(2):
            z1(w, d, 0).start()

    to_east.wait_recv()
    to_west.wait_recv()

    def place(q):
        for side, lo in ((0, 4), (1, 16)):
            v = crecv[side, q].astype(f32)
            for i in range(4):
                for t in range(tiles):
                    xpad[t, 4 * q + i, lo : lo + 4, :] = v[4 * i : 4 * i + 4, t * 128 : (t + 1) * 128]

    def place_loop(q, _):
        place(q)
        return 0

    lax.fori_loop(1, last + 2, place_loop, 0)

    def margin(present, copies, row0, q, slot):
        @pl.when(present)
        def _():
            for c in copies:
                c.wait_recv()
            place(q)
            for r in range(3):
                v = rrecv[slot, r].astype(f32)
                for t in range(tiles):
                    xpad[t, row0 + r, 8:16, :] = v[:, t * 128 : (t + 1) * 128]

        @pl.when(jnp.logical_not(present))
        def _():
            for r in range(3):
                for t in range(tiles):
                    xpad[t, row0 + r] = jnp.zeros((24, 128), f32)

    margin(has_up, to_down, 1, 0, 0)
    margin(has_down, to_up, rows + 4, last + 2, 1)

    def conv_tile(rb, t):
        lanes = pl.ds(pl.multiple_of(t * 128, 128), 128)
        acc = [jnp.broadcast_to(dbias[:, lanes], (8, 128)) for _ in range(8)]
        for b in range(7):
            win = [xpad[t, rb * 8 + 1 + r, 5 + b : 13 + b, :] for r in range(14)]
            for a in range(7):
                k = jnp.broadcast_to(kers[a, b : b + 1, lanes], (8, 128))
                for o in range(8):
                    acc[o] = acc[o] + win[o + a] * k
        for o in range(8):
            conv[pl.ds(pl.multiple_of((rb * 8 + o) * 8, 8), 8), lanes] = acc[o]

    def norm_group(rb, g):
        px = pl.ds(pl.multiple_of(rb * chunk + g * 16, 16), 16)
        v = conv[px, :]
        v = v - jnp.mean(v, axis=-1, keepdims=True)
        var = jnp.mean(v * v, axis=-1, keepdims=True)
        v = v * lax.rsqrt(var + 1e-06) * gain[...] + nbias[...]
        acts[lat, px, :] = v.astype(bf16)

    def act(slot, c):
        return acts.at[slot, pl.ds(pl.multiple_of(c * chunk, chunk), chunk), :]

    def a_sib(c):
        return remote(act(lat, c), act(lat, c), a_ss.at[0, c], a_rs.at[0, c], sib)

    def a_crs(c):
        return remote(act(lat, c), act(lat, c), a_ss.at[1, c], a_rs.at[1, c], crs)

    def a_fwd(c):
        return remote(act(far, c), act(far, c), a_ss.at[2, c], a_rs.at[2, c], sib)

    def conv_block(rb, _):
        def run(t, _):
            conv_tile(rb, t)
            return 0

        lax.fori_loop(0, tiles // 2, run, 0)
        serve(0, rb)
        lax.fori_loop(tiles // 2, tiles, run, 0)

        def run_norm(g, _):
            norm_group(rb, g)
            return 0

        lax.fori_loop(0, chunk // 16, run_norm, 0)
        a_crs(rb).start()
        a_sib(rb).start()
        serve(1, rb)
        return 0

    lax.fori_loop(0, blocks, conv_block, 0)

    def forward(c):
        a_crs(c).wait_recv()
        a_fwd(c).start()

    pending = list(range(blocks))
    for s in range(blocks, STEPS):
        for w in range(2):
            if s < STEPS - 2:
                serve(w, s)
            elif s == STEPS - 2:
                serve_end(w)
            else:
                serve_last(w)
            if w == 0 and pending:
                forward(pending.pop(0))
    for c in pending:
        forward(c)

    for k in range(1, NX):
        whole(0, k).wait_recv()

    def pointwise(q):
        def one(n, _):
            lanes = pl.ds(pl.multiple_of(n * 256, 256), 256)
            wt = wts[0, :, :, lanes].reshape(chans, 256)
            pre = jnp.dot(acts[q], wt, preferred_element_type=f32) + ubias[:, lanes]
            act_ = 0.5 * pre * (1.0 + lax.erf(pre * 0.7071067811865476))
            hid[:, lanes] = act_.astype(bf16)
            return 0

        lax.fori_loop(0, hidden // 256, one, 0)

    def project(n):
        return lax.dot_general(hid[...], wts[1, n], (((1,), (1,)), ((), ())), preferred_element_type=f32)

    def o_copy(kind, n):
        src, dst, device = ((s_sib, r_sib, sib), (s_mid, r_mid, crs), (s_crs, r_crs, sib))[kind]
        return remote(src.at[n], dst.at[n], o_ss.at[kind, n], o_rs.at[kind, n], device)

    parts = NX
    for c in range(blocks):
        a_sib(c).wait_recv()
        a_fwd(c).wait_recv()

    pointwise(far_flip)
    for k in range(1, NX):
        whole(1, k).wait_recv()

    def first_part(n, _):
        s_sib[n] = project(n).astype(bf16)
        o_copy(0, n).start()
        return 0

    lax.fori_loop(0, parts, first_part, 0)

    pointwise(far)

    def second_part(n, _):
        total = project(n)
        o_copy(0, n).wait_recv()
        s_mid[n] = (total + r_sib[n].astype(f32)).astype(bf16)
        o_copy(1, n).start()
        return 0

    lax.fori_loop(0, parts, second_part, 0)

    pointwise(flip)

    def third_part(n, _):
        s_crs[n] = project(n).astype(bf16)
        o_copy(2, n).start()
        return 0

    lax.fori_loop(0, parts, third_part, 0)

    pointwise(lat)

    def own_part(n, _):
        own[n] = project(n)
        return 0

    lax.fori_loop(0, parts, own_part, 0)

    def finish(n, _):
        width = chans // parts
        lanes = pl.ds(pl.multiple_of(n * width, width), width)
        o_copy(2, n).wait_recv()
        part = own[n] + r_crs[n].astype(f32)
        o_copy(1, n).wait_recv()
        part = part + r_mid[n].astype(f32)
        part = scale[:, lanes] * (part + obias[:, lanes])
        res = feat[:, :, lanes].astype(f32) + part.reshape(rows, cols, width)
        out[:, :, lanes] = res.astype(bf16)
        return 0

    lax.fori_loop(0, parts, finish, 0)

    for w in range(2):
        ycopy[w].wait_send()
        for k in range(1, NX):
            x1(w, k).wait_send()
            whole(w, k).wait_send()
        for d in range(2):

            def gone(s, _, w=w, d=d):
                z1(w, d, s).wait_send()
                z2(w, d, s).wait_send()
                return 0

            lax.fori_loop(0, length(w, d), gone, 0)
    to_east.wait_send()
    to_west.wait_send()

    @pl.when(has_down)
    def _():
        for c in to_down:
            c.wait_send()

    @pl.when(has_up)
    def _():
        for c in to_up:
            c.wait_send()

    for c in range(blocks):
        a_sib(c).wait_send()
        a_crs(c).wait_send()
        a_fwd(c).wait_send()
    for n in range(parts):
        for kind in range(3):
            o_copy(kind, n).wait_send()


def local(
    features, depth_kernel, depth_bias, norm_gain, norm_bias, up_weight, up_bias, down_weight, down_bias, layer_scale
):
    rows, cols, chans = features.shape
    shard, hidden = up_weight.shape
    pixels = rows * cols
    bf16, f32 = jnp.bfloat16, jnp.float32
    vmem, dma = pltpu.VMEM, pltpu.SemaphoreType.DMA
    blocks = rows // 8
    flat = lambda v: v.reshape(1, -1)
    spec = pl.BlockSpec(memory_space=pltpu.VMEM)
    piece = (NX, pixels, chans // NX)
    return pl.pallas_call(
        kernel,
        out_shape=jax.ShapeDtypeStruct(features.shape, features.dtype),
        in_specs=[spec] * 10,
        out_specs=spec,
        scratch_shapes=[
            vmem((2, NX, chans // NX, hidden), bf16),
            vmem((2, shard, hidden), bf16),
            vmem((chans // 128, rows + 8, 24, 128), f32),
            vmem((7, 8, chans), f32),
            vmem((pixels, chans), f32),
            vmem((2, rows // 4, 16, chans), bf16),
            vmem((2, rows // 4 + 2, 16, chans), bf16),
            vmem((2, 3, cols, chans), bf16),
            vmem((4, pixels, chans), bf16),
            vmem((pixels, hidden), bf16),
            vmem(piece, f32),
            vmem(piece, bf16),
            vmem(piece, bf16),
            vmem(piece, bf16),
            vmem(piece, bf16),
            vmem(piece, bf16),
            vmem(piece, bf16),
            dma((2,)), dma((2,)),
            dma((8,)), dma((8,)),
            dma((2, NX - 1)), dma((2, NX - 1)),
            dma((2, NX - 1)), dma((2, NX - 1)),
            dma((2, 2, STEPS)), dma((2, 2, STEPS)),
            dma((2, 2, STEPS)), dma((2, 2, STEPS)),
            dma((3, blocks)), dma((3, blocks)),
            dma((3, NX)), dma((3, NX)),
        ],
        compiler_params=pltpu.CompilerParams(
            collective_id=0, has_side_effects=True, vmem_limit_bytes=48 << 20
        ),
    )(
        features, depth_kernel, flat(depth_bias), flat(norm_gain), flat(norm_bias), up_weight, flat(up_bias),
        down_weight, flat(down_bias), flat(layer_scale),
    )


def solution(mesh):
    placed = (
        P("lat", "lon", None), P(), P(), P(), P(), P("lon", "lat"), P("lat"), P("lon", "lat"), P(), P(),
    )
    return jax.shard_map(
        local, mesh=mesh, in_specs=placed, out_specs=P("lat", "lon", None), check_vma=False
    )
```

time: 1330 us -> 86.7 us (0.07)
  waiting for transfers between devices: 1260 us -> 0 us
  Pallas kernels: 0 us -> 78.4 us
  starting transfers between devices: 25.1 us -> 0 us
  matrix products: 16.1 us -> 0 us
  other arithmetic: 13.5 us -> 0 us
    all_gather x3 -> x0, waiting for transfers between devices: 1120 us -> none  [the longest x1 582 us: local(): lax.all_gather(down_weight, 'lon', axis=0, tiled=True)]
    reduce_scatter x1 -> x0, waiting for transfers between devices: 132 us -> none  [local(): lax.psum_scatter(partial_out.astype(jnp.bfloat16), 'lat', scatter_dimensi...]
    pallas_call x0 -> x1, Pallas kernels: none -> 78.4 us  [local(): pl.pallas_call(kernel, out_shape=jax.ShapeDtypeStruct(features.shape, fea...]
    ppermute x4 -> x0, starting transfers between devices: 25 us -> none  [the longest x2 15 us: with_halo(): lax.ppermute(lax.slice_in_dim(block, 0, width, axis=dim), axis, backward)]
    dot_general x1 -> x0, matrix products: 16.1 us -> none  [local(): lax.dot_general(hidden, lax.all_gather(down_weight, 'lon', axis=0, tiled=...]
  transfers between devices with their start and end apart: 8 -> 0, of which waited for: 6 -> 0; matrix products, arithmetic and copies ran while one was open for 0% -> 0% of each run, Pallas kernels for 0% -> 0%
where the time goes in v2:
time: 86.7 us; the launch traced here: 86.1 us
  Pallas kernels  78.4 us (90%)
  local copies, waits for them, and re-layouts  7.61 us (9%)
    pallas_call x1, Pallas kernels, local(): pl.pallas_call(kernel, out_shape=jax.ShapeDtypeStruct(features.shape, fea...  78.4 us
    unnamed x21, local copies, waits for them, and re-layouts  7.61 us

profile of v2, /device:TPU:1, one launch (start us, length us, event | category | flops | bytes accessed | tf_op | source)
XLA Modules:
  0.0 86.1 jit_solution(4650731616278791294)
XLA Ops:
  0.0 0.0 copy-start.5
  0.0 0.0 copy-start.4
  0.0 0.7 copy-done.5
  0.7 0.0 copy-done.4
  0.7 0.0 copy-start
  0.7 1.0 %copy-done = bf16[32,8,1024]{2,1,0:T(8,128)(2,1)S(1)} copy-done((bf16[32,8,1024]{2,1,0:T(8,128)(2,1)S(1)}, bf16[32,8,1024]{2,1,0:T(8,128)(2,1)}, u32[]{:S(2)}) %copy-start) | copy-done | bytes 524312
  1.7 0.0 copy-start.1
  1.7 0.9 %copy-done.1 = bf16[7,7,1024]{2,1,0:T(8,128)(2,1)S(1)} copy-done((bf16[7,7,1024]{2,1,0:T(8,128)(2,1)S(1)}, bf16[7,7,1024]{2,1,0:T(8,128)(2,1)}, u32[]{:S(2)}) %copy-start.1) | copy-done | bytes 100376
  2.6 0.0 copy-start.2
  2.6 0.7 copy-done.2
  3.4 0.0 copy-start.3
  3.4 0.7 copy-done.3
  4.1 0.0 copy-start.6
  4.1 0.7 copy-done.6
  4.8 0.0 copy-start.7
  4.8 0.7 copy-done.7
  5.5 0.0 copy-start.8
  5.5 0.7 copy-done.8
  6.1 0.0 copy-start.9
  6.1 0.7 copy-done.9
  6.8 78.4 %shard_map.100 = bf16[32,8,1024]{2,1,0:T(8,128)(2,1)S(1)} custom-call(bf16[32,8,1024]{2,1,0:T(8,128)(2,1)S(1)} %copy-done, bf16[7,7,1024]{2,1,0:T(8,128)(2,1)S(1)} %copy-done.1, f32[1,1024]{1,0:T(1,128)S(1)} %bitcast.6, f32[1,1024]{1,0:T(1,128)S(1)} %bitcast.7, f32[1,1024]{1,0:T(1,128)S(1)} %bitcast.8, bf16[8,1024]{1,0:T(8,128)(2,1)S(1)} %copy-done.2, ...), custom_call_target="tpu_custom_call" | custom-call | tf_op jit(solution)/shard_map/pallas_call | solution.py:455
  85.3 0.8 copy.12
Async XLA Ops:
  0.0 0.7 copy-start.5
  0.0 0.7 copy-start.4
  0.7 1.0 %copy-start = (bf16[32,8,1024]{2,1,0:T(8,128)(2,1)S(1)}, bf16[32,8,1024]{2,1,0:T(8,128)(2,1)}, u32[]{:S(2)}) copy-start(bf16[32,8,1024]{2,1,0:T(8,128)(2,1)} %feat.1) | copy-start | bytes 1572868
  1.7 0.9 %copy-start.1 = (bf16[7,7,1024]{2,1,0:T(8,128)(2,1)S(1)}, bf16[7,7,1024]{2,1,0:T(8,128)(2,1)}, u32[]{:S(2)}) copy-start(bf16[7,7,1024]{2,1,0:T(8,128)(2,1)} %dker.1) | copy-start | bytes 301060
  2.6 0.7 copy-start.2
  3.4 0.7 copy-start.3
  4.1 0.7 copy-start.6
  4.8 0.7 copy-start.7
  5.5 0.7 copy-start.8
  6.1 0.7 copy-start.9

commit v3 on v2

v3 whole, which is shorter than its diff:
```python
import functools

import jax
import jax.numpy as jnp
from jax import lax
from jax.experimental import pallas as pl
from jax.experimental.pallas import tpu as pltpu
from jax.sharding import PartitionSpec as P

MESH = pl.DeviceIdType.MESH
NX, NZ, NY = 4, 16, 2
STEPS = NZ // 2
EARLY = 1
DIRECT = STEPS - 2


def remote(src, dst, send_sem, recv_sem, device):
    return pltpu.make_async_remote_copy(
        src_ref=src, dst_ref=dst, send_sem=send_sem, recv_sem=recv_sem, device_id=device, device_id_type=MESH
    )


def kernel(
    feat_h, dker_h, dbias_h, gain_h, nbias_h, up, ubias_h, down, obias_h, scale_h,
    out,
    feat, dker, dbias, gain, nbias, ubias, obias, scale,
    wts, xpad, kers, conv, csend, crecv, rrecv, acts, hid, own, s_sib, s_mid, s_crs, r_sib, r_mid, r_crs,
    in_s, own_s, y_ss, y_rs, h_ss, h_rs, hc_ss, hc_rs, x1_ss, x1_rs, x2_ss, x2_rs, xf_ss, xf_rs, z1_ss, z1_rs, z2_ss, z2_rs, a_ss, a_rs, o_ss, o_rs,
):
    f32, bf16 = jnp.float32, jnp.bfloat16
    rows, cols, chans = feat.shape
    hidden = up.shape[1]
    tiles = chans // 128
    wide_l = hidden // 4
    thin_l = hidden - wide_l
    blocks = rows // 8
    chunk = 8 * cols
    pixels = rows * cols
    n_lon = NX * NZ * NY
    lat = lax.axis_index("lat")
    lon = lax.axis_index("lon")
    y = lax.rem(lon, NY)
    z = lax.rem(lon // NY, NZ)
    x = lon // (NY * NZ)

    def at(x_, z_, y_=y):
        return (lat, (lax.rem(x_ + NX, NX) * NZ + lax.rem(z_ + NZ, NZ)) * NY + y_)

    flip = lat + 1 - 2 * lax.rem(lat, 2)
    far = lax.rem(lat + 2, 4)
    far_flip = lax.rem(flip + 2, 4)
    pair_lon = lon + 1 - 2 * y
    pair = (lat, pair_lon)
    sib = (flip, lon)
    crs = (far, pair_lon)
    east = lax.rem(lon + 1, n_lon)
    west = lax.rem(lon + n_lon - 1, n_lon)
    has_up = lat > 0
    has_down = lat < 3

    barrier = pltpu.get_barrier_semaphore()

    def hello(device):
        pl.semaphore_signal(barrier, inc=1, device_id=device, device_id_type=MESH)

    near = [pair, sib, crs, (lat, east), (lat, west), at(x, z + 1), at(x, z - 1)]
    near += [at(x + k, z, y_) for k in range(1, NX) for y_ in (y, 1 - y)]
    for device in near:
        hello(device)

    @pl.when(has_up)
    def _():
        for lon_ in (west, lon, east):
            hello((lat - 1, lon_))

    @pl.when(has_down)
    def _():
        for lon_ in (west, lon, east):
            hello((lat + 1, lon_))

    shard = up.shape[0]
    mine = pl.ds(pl.multiple_of((z * NY + y) * shard, shard), shard)
    own_copy = [pltpu.make_async_copy((up, down)[w], wts.at[w, x, mine, :], own_s.at[w]) for w in range(2)]
    loads = [
        pltpu.make_async_copy(a, b, in_s.at[i])
        for i, (a, b) in enumerate(
            (
                (feat_h, feat), (dker_h, dker), (dbias_h, dbias), (gain_h, gain),
                (nbias_h, nbias), (ubias_h, ubias), (obias_h, obias), (scale_h, scale),
            )
        )
    ]
    for c in own_copy + loads:
        c.start()
    pl.semaphore_wait(barrier, len(near) + 3 * has_up.astype(jnp.int32) + 3 * has_down.astype(jnp.int32))

    def y_copy(w):
        return remote((up, down)[w], wts.at[w, x, mine, :], y_ss.at[w], y_rs.at[w], pair)

    def x1(w, k, i):
        src = (up, down)[w].at[:, pl.ds(0, wide_l)]
        dst = wts.at[w, x, mine, pl.ds(0, wide_l)]
        return remote(src, dst, x1_ss.at[w, k - 1, i], x1_rs.at[w, k - 1, i], at(x + k, z, (y, 1 - y)[i]))

    for w in range(2):
        y_copy(w).start()
        for k in range(1, NX):
            for i in range(2):
                x1(w, k, i).start()

    prow = NY * shard

    def wide(w, zb):
        return wts.at[w, :, pl.ds(pl.multiple_of(zb * prow, prow), prow), pl.ds(0, wide_l)]

    def thin(w, xb, zb):
        return wts.at[w, xb, pl.ds(pl.multiple_of(zb * prow, prow), prow), pl.ds(wide_l, thin_l)]

    def length(w, d):
        return STEPS if w == d else STEPS - 1

    def block(d, s):
        return lax.rem(z + (NZ - s if d == 0 else s), NZ)

    def z1(w, d, s):
        ref = wide(w, block(d, s))
        return remote(ref, ref, z1_ss.at[w, d, s], z1_rs.at[w, d, s], at(x, z + 1 if d == 0 else z - 1))

    def z2(w, d, s):
        ref = thin(w, x, block(d, s))
        return remote(ref, ref, z2_ss.at[w, d, s], z2_rs.at[w, d, s], at(x, z + 1 if d == 0 else z - 1))

    def slot_block(d, s, own_slot):
        return jnp.where(own_slot, z, block(d, s + 1)) if not isinstance(own_slot, bool) else (
            z if own_slot else block(d, s + 1)
        )

    def x2(w, e, d, s, own_slot=False):
        ref = thin(w, x, slot_block(d, s, own_slot))
        return remote(ref, ref, x2_ss.at[w, e], x2_rs.at[w, e, d, s], at(x + 1 - 2 * e, z))

    def xf(w, d, s, own_slot=False):
        ref = thin(w, lax.rem(x + (NX - 1 if d == 0 else 1), NX), slot_block(d, s, own_slot))
        return remote(ref, ref, xf_ss.at[w], xf_rs.at[w], at(x + 1 - 2 * d, z))

    def xd(w, d, s):
        ref = thin(w, x, block(d, s + 1))
        return remote(ref, ref, xf_ss.at[w], xf_rs.at[w], at(x + 2, z))

    def bulk(w, ss, rs):
        ref = wts.at[w, 0, :, pl.ds(wide_l, thin_l)]
        return remote(ref, ref, ss, rs, at(x + 1, z))

    for c in loads[:2]:
        c.wait()
    for a in range(7):
        kers[a, 0:7, :] = dker[a].astype(f32)
    low4 = lax.broadcasted_iota(jnp.int32, (8, chans), 0) < 4

    def pack(q, _):
        v = [feat[4 * q + i].astype(f32) for i in range(4)]
        turned = [pltpu.roll(t, 4, 0) for t in v]
        right = [jnp.where(low4, turned[i], v[i + 1]) for i in (0, 2)]
        left = [jnp.where(low4, v[i], turned[i + 1]) for i in (0, 2)]
        csend[0, q] = jnp.concatenate(right, 0).astype(bf16)
        csend[1, q] = jnp.concatenate(left, 0).astype(bf16)
        return 0

    lax.fori_loop(0, rows // 4, pack, 0)

    last = rows // 4 - 1

    def h_copy(side, c):
        src = csend.at[side, pl.ds(2 * c, 2)]
        dst = crecv.at[side, pl.ds(2 * c + 1, 2)]
        return remote(src, dst, hc_ss.at[side, c], hc_rs.at[side, c], (lat, (east, west)[side]))

    to_down = [
        remote(feat.at[pl.ds(rows - 3, 3)], rrecv.at[0], h_ss.at[0], h_rs.at[0], (lat + 1, lon)),
        remote(csend.at[0, last], crecv.at[0, 0], h_ss.at[1], h_rs.at[1], (lat + 1, east)),
        remote(csend.at[1, last], crecv.at[1, 0], h_ss.at[2], h_rs.at[2], (lat + 1, west)),
    ]
    to_up = [
        remote(feat.at[pl.ds(0, 3)], rrecv.at[1], h_ss.at[3], h_rs.at[3], (lat - 1, lon)),
        remote(csend.at[0, 0], crecv.at[0, last + 2], h_ss.at[4], h_rs.at[4], (lat - 1, east)),
        remote(csend.at[1, 0], crecv.at[1, last + 2], h_ss.at[5], h_rs.at[5], (lat - 1, west)),
    ]

    for c in own_copy:
        c.wait()
    for w in range(2):
        y_copy(w).wait_recv()
        for d in range(2):
            z2(w, d, 0).start()
        for e in range(2):
            x2(w, e, 1 - w, STEPS - 1, True).start()
    for c in range(2):
        for side in range(2):
            h_copy(side, c).start()

    @pl.when(has_down)
    def _():
        for c in to_down:
            c.start()

    @pl.when(has_up)
    def _():
        for c in to_up:
            c.start()

    def widen(h, _):
        v = feat[h].astype(f32)
        for t in range(tiles):
            xpad[t, h + 4, 8:16, :] = v[:, t * 128 : (t + 1) * 128]
        return 0

    lax.fori_loop(0, rows, widen, 0)

    def thin_step(w, s):
        for d in range(2):
            if isinstance(s, int) and s >= length(w, d):
                continue
            z2(w, d, s).wait_recv()
            if not isinstance(s, int) or s + 1 < length(w, d):
                z2(w, d, s + 1).start()
            for e in range(2):
                x2(w, e, d, s).start()
            if isinstance(s, int) and s >= DIRECT:
                xd(w, d, s).start()
        if isinstance(s, int) and s == 0:
            x2(w, 1 - w, 1 - w, STEPS - 1, True).wait_recv()
            xf(w, 1 - w, STEPS - 1, True).start()
        elif not isinstance(s, int) or s <= DIRECT:
            for d in range(2):
                cross_step(w, d, s - 1)

    def cross_step(w, d, s):
        x2(w, d, d, s).wait_recv()
        xf(w, d, s).start()

    def wide_step(w, s):
        for d in range(2):
            if isinstance(s, int) and s >= length(w, d):
                continue
            z1(w, d, s).wait_recv()
            if not isinstance(s, int) or s + 1 < length(w, d):
                z1(w, d, s + 1).start()

    def gathered(w):
        for d in range(2):

            def one(s, _, d=d):
                x2(w, 1 - d, d, s).wait_recv()
                return 0

            lax.fori_loop(0, STEPS, one, 0)
            for s in range(DIRECT, length(w, d)):
                x2(w, d, d, s).wait_recv()
        bulk(w, xf_ss.at[w], xf_rs.at[w]).wait_recv()

    for w in range(2):
        for k in range(1, NX):
            for i in range(2):
                x1(w, k, i).wait_recv()
        for d in range(2):
            z1(w, d, 0).start()
    for side in range(2):
        h_copy(side, 2).start()
    for s in range(EARLY + 1):
        for w in range(2):
            thin_step(w, s)
            if s > 0:
                wide_step(w, s - 1)
        if s == 0:
            for side in range(2):
                h_copy(side, 3).start()
    for c in loads[2:]:
        c.wait()

    def place(q):
        for side, lo in ((0, 4), (1, 16)):
            v = crecv[side, q].astype(f32)
            for i in range(4):
                for t in range(tiles):
                    xpad[t, 4 * q + i, lo : lo + 4, :] = v[4 * i : 4 * i + 4, t * 128 : (t + 1) * 128]

    def chunk_in(c):
        for side in range(2):
            h_copy(side, c).wait_recv()

        def one(i, _):
            place(2 * c + 1 + i)
            return 0

        lax.fori_loop(0, 2, one, 0)

    chunk_in(0)

    def margin(present, copies, row0, q, slot):
        @pl.when(present)
        def _():
            for c in copies:
                c.wait_recv()
            place(q)
            for r in range(3):
                v = rrecv[slot, r].astype(f32)
                for t in range(tiles):
                    xpad[t, row0 + r, 8:16, :] = v[:, t * 128 : (t + 1) * 128]

        @pl.when(jnp.logical_not(present))
        def _():
            for r in range(3):
                for t in range(tiles):
                    xpad[t, row0 + r] = jnp.zeros((24, 128), f32)

    margin(has_up, to_down, 1, 0, 0)

    def conv_tile(rb, t):
        lanes = pl.ds(pl.multiple_of(t * 128, 128), 128)
        acc = [jnp.broadcast_to(dbias[:, lanes], (8, 128)) for _ in range(8)]
        for b in range(7):
            win = [xpad[t, rb * 8 + 1 + r, 5 + b : 13 + b, :] for r in range(14)]
            for a in range(7):
                k = jnp.broadcast_to(kers[a, b : b + 1, lanes], (8, 128))
                for o in range(8):
                    acc[o] = acc[o] + win[o + a] * k
        for o in range(8):
            conv[pl.ds(pl.multiple_of((rb * 8 + o) * 8, 8), 8), lanes] = acc[o]

    def norm_group(rb, g):
        px = pl.ds(pl.multiple_of(rb * chunk + g * 16, 16), 16)
        v = conv[px, :]
        v = v - jnp.mean(v, axis=-1, keepdims=True)
        var = jnp.mean(v * v, axis=-1, keepdims=True)
        v = v * lax.rsqrt(var + 1e-06) * gain[...] + nbias[...]
        acts[lat, px, :] = v.astype(bf16)

    def act(slot, c):
        return acts.at[slot, pl.ds(pl.multiple_of(c * chunk, chunk), chunk), :]

    def a_sib(c):
        return remote(act(lat, c), act(lat, c), a_ss.at[0, c], a_rs.at[0, c], sib)

    def a_crs(c):
        return remote(act(lat, c), act(lat, c), a_ss.at[1, c], a_rs.at[1, c], crs)

    def a_fwd(c):
        return remote(act(far, c), act(far, c), a_ss.at[2, c], a_rs.at[2, c], sib)

    def conv_block(rb, _):
        @pl.when(rb < blocks - 1)
        def _():
            chunk_in(rb + 1)

        @pl.when(rb == blocks - 1)
        def _():
            margin(has_down, to_up, rows + 4, last + 2, 1)

        def run(t, _):
            conv_tile(rb, t)
            return 0

        lax.fori_loop(0, tiles // 2, run, 0)
        thin_step(0, rb + EARLY + 1)
        wide_step(0, rb + EARLY)
        lax.fori_loop(tiles // 2, tiles, run, 0)

        def run_norm(g, _):
            norm_group(rb, g)
            return 0

        lax.fori_loop(0, chunk // 16, run_norm, 0)
        a_crs(rb).start()
        a_sib(rb).start()
        thin_step(1, rb + EARLY + 1)
        wide_step(1, rb + EARLY)
        return 0

    lax.fori_loop(0, blocks, conv_block, 0)

    def forward(c):
        a_crs(c).wait_recv()
        a_fwd(c).start()

    pending = list(range(blocks))
    for s in range(EARLY + blocks, STEPS + 1):
        for w in range(2):
            if s + 1 < STEPS:
                thin_step(w, s + 1)
            if s < STEPS:
                wide_step(w, s)
            if w == 0 and pending:
                forward(pending.pop(0))
    for c in pending:
        forward(c)
    gathered(0)

    def pointwise(q, h):
        def one(n, _):
            lanes = pl.ds(pl.multiple_of(n * 256, 256), 256)
            wt = wts[0, :, :, lanes].reshape(chans, 256)
            pre = jnp.dot(acts[q], wt, preferred_element_type=f32) + ubias[:, lanes]
            act_ = 0.5 * pre * (1.0 + lax.erf(pre * 0.7071067811865476))
            hid[h, :, lanes] = act_.astype(bf16)
            return 0

        lax.fori_loop(0, hidden // 256, one, 0)

    def project(n, h):
        return lax.dot_general(hid[h], wts[1, n], (((1,), (1,)), ((), ())), preferred_element_type=f32)

    def o_copy(kind, n):
        src, dst, device = ((s_sib, r_sib, sib), (s_mid, r_mid, crs), (s_crs, r_crs, sib))[kind]
        return remote(src.at[n], dst.at[n], o_ss.at[kind, n], o_rs.at[kind, n], device)

    parts = NX
    for c in range(blocks):
        a_sib(c).wait_recv()
        a_fwd(c).wait_recv()

    pointwise(far_flip, 0)
    pointwise(far, 1)
    gathered(1)

    def first_part(n):
        s_sib[n] = project(n, 0).astype(bf16)
        o_copy(0, n).start()

    def second_part(n):
        total = project(n, 1)
        o_copy(0, n).wait_recv()
        s_mid[n] = (total + r_sib[n].astype(f32)).astype(bf16)
        o_copy(1, n).start()

    first_part(0)

    def both_parts(n, _):
        first_part(n + 1)
        second_part(n)
        return 0

    lax.fori_loop(0, parts - 1, both_parts, 0)
    second_part(parts - 1)

    pointwise(flip, 0)

    def third_part(n, _):
        s_crs[n] = project(n, 0).astype(bf16)
        o_copy(2, n).start()
        return 0

    lax.fori_loop(0, parts, third_part, 0)

    pointwise(lat, 1)

    def own_part(n, _):
        own[n] = project(n, 1)
        return 0

    lax.fori_loop(0, parts, own_part, 0)

    def finish(n, _):
        width = chans // parts
        lanes = pl.ds(pl.multiple_of(n * width, width), width)
        o_copy(2, n).wait_recv()
        part = own[n] + r_crs[n].astype(f32)
        o_copy(1, n).wait_recv()
        part = part + r_mid[n].astype(f32)
        part = scale[:, lanes] * (part + obias[:, lanes])
        res = feat[:, :, lanes].astype(f32) + part.reshape(rows, cols, width)
        out[:, :, lanes] = res.astype(bf16)
        return 0

    lax.fori_loop(0, parts, finish, 0)

    for w in range(2):
        y_copy(w).wait_send()
        for k in range(1, NX):
            for i in range(2):
                x1(w, k, i).wait_send()
        for e in range(2):
            bulk(w, x2_ss.at[w, e], xf_rs.at[w]).wait_send()
        bulk(w, xf_ss.at[w], xf_rs.at[w]).wait_send()
        for d in range(2):

            def gone(s, _, w=w, d=d):
                z1(w, d, s).wait_send()
                z2(w, d, s).wait_send()
                return 0

            lax.fori_loop(0, length(w, d), gone, 0)
    for side in range(2):
        for c in range(blocks):
            h_copy(side, c).wait_send()

    @pl.when(has_down)
    def _():
        for c in to_down:
            c.wait_send()

    @pl.when(has_up)
    def _():
        for c in to_up:
            c.wait_send()

    for c in range(blocks):
        a_sib(c).wait_send()
        a_crs(c).wait_send()
        a_fwd(c).wait_send()
    for n in range(parts):
        for kind in range(3):
            o_copy(kind, n).wait_send()


def local(
    features, depth_kernel, depth_bias, norm_gain, norm_bias, up_weight, up_bias, down_weight, down_bias, layer_scale
):
    rows, cols, chans = features.shape
    shard, hidden = up_weight.shape
    pixels = rows * cols
    bf16, f32 = jnp.bfloat16, jnp.float32
    vmem, dma = pltpu.VMEM, pltpu.SemaphoreType.DMA
    blocks = rows // 8
    flat = lambda v: v.reshape(1, -1)
    spec = pl.BlockSpec(memory_space=pltpu.VMEM)
    piece = (NX, pixels, chans // NX)
    return pl.pallas_call(
        kernel,
        out_shape=jax.ShapeDtypeStruct(features.shape, features.dtype),
        in_specs=[pl.BlockSpec(memory_space=pltpu.HBM)] * 10,
        out_specs=spec,
        scratch_shapes=[
            vmem(features.shape, bf16),
            vmem(depth_kernel.shape, bf16),
            vmem((1, chans), f32),
            vmem((1, chans), f32),
            vmem((1, chans), f32),
            vmem((1, hidden), f32),
            vmem((1, chans), f32),
            vmem((1, chans), f32),
            vmem((2, NX, chans // NX, hidden), bf16),
            vmem((chans // 128, rows + 8, 24, 128), f32),
            vmem((7, 8, chans), f32),
            vmem((pixels, chans), f32),
            vmem((2, rows // 4, 16, chans), bf16),
            vmem((2, rows // 4 + 2, 16, chans), bf16),
            vmem((2, 3, cols, chans), bf16),
            vmem((4, pixels, chans), bf16),
            vmem((2, pixels, hidden), bf16),
            vmem(piece, f32),
            vmem(piece, bf16),
            vmem(piece, bf16),
            vmem(piece, bf16),
            vmem(piece, bf16),
            vmem(piece, bf16),
            vmem(piece, bf16),
            dma((8,)), dma((2,)),
            dma((2,)), dma((2,)),
            dma((6,)), dma((6,)),
            dma((2, blocks)), dma((2, blocks)),
            dma((2, NX - 1, 2)), dma((2, NX - 1, 2)),
            dma((2, 2)), dma((2, 2, 2, STEPS)),
            dma((2,)), dma((2,)),
            dma((2, 2, STEPS)), dma((2, 2, STEPS)),
            dma((2, 2, STEPS)), dma((2, 2, STEPS)),
            dma((3, blocks)), dma((3, blocks)),
            dma((3, NX)), dma((3, NX)),
        ],
        compiler_params=pltpu.CompilerParams(
            collective_id=0, has_side_effects=True, vmem_limit_bytes=63 << 20
        ),
    )(
        features, depth_kernel, flat(depth_bias), flat(norm_gain), flat(norm_bias), up_weight, flat(up_bias),
        down_weight, flat(down_bias), flat(layer_scale),
    )


def solution(mesh):
    placed = (
        P("lat", "lon", None), P(), P(), P(), P(), P("lon", "lat"), P("lat"), P("lon", "lat"), P(), P(),
    )
    return jax.shard_map(
        local, mesh=mesh, in_specs=placed, out_specs=P("lat", "lon", None), check_vma=False
    )
```

time: 86.7 us -> 79.9 us (0.922)
  local copies, waits for them, and re-layouts: 7.61 us -> 1.87 us
    unnamed x21 -> x1, local copies, waits for them, and re-layouts: 7.61 us -> 1.87 us
where the time goes in v3:
time: 79.9 us; the launch traced here: 79.8 us
  Pallas kernels  77.9 us (97%)
  local copies, waits for them, and re-layouts  1.87 us (2%)
    pallas_call x1, Pallas kernels, local(): pl.pallas_call(kernel, out_shape=jax.ShapeDtypeStruct(features.shape, fea...  77.9 us
    unnamed x1, local copies, waits for them, and re-layouts  1.87 us

profile of v3, /device:TPU:1, one launch (start us, length us, event | category | flops | bytes accessed | tf_op | source)
XLA Modules:
  0.0 79.8 jit_solution(17171637845458043014)
XLA Ops:
  0.0 77.9 %shard_map.100 = bf16[32,8,1024]{2,1,0:T(8,128)(2,1)} custom-call(bf16[32,8,1024]{2,1,0:T(8,128)(2,1)} %feat_h.1, bf16[7,7,1024]{2,1,0:T(8,128)(2,1)} %dker_h.1, f32[1,1024]{1,0:T(1,128)} %bitcast.6, f32[1,1024]{1,0:T(1,128)} %bitcast.7, f32[1,1024]{1,0:T(1,128)} %bitcast.8, bf16[8,1024]{1,0:T(8,128)(2,1)} %up.1, f32[1,1024]{1,0:T(1,128)} %bitcast.9, ...), custom_call_target="tpu_custom_call" | custom-call | tf_op jit(solution)/shard_map/pallas_call | solution.py:527
  77.9 1.9 %copy.12 = bf16[32,8,1024]{2,1,0:T(8,128)(2,1)} copy(bf16[32,8,1024]{2,1,0:T(8,128)(2,1)} %shard_map.100) | data formatting | bytes 1048576

commit v4 on v3

--- a/solution.py
+++ b/solution.py
@@ -10,7 +10,7 @@
 MESH = pl.DeviceIdType.MESH
 NX, NZ, NY = 4, 16, 2
 STEPS = NZ // 2
-EARLY = 1
+HOPS = STEPS // 2
 DIRECT = STEPS - 2
 
 
@@ -31,7 +31,7 @@
     rows, cols, chans = feat.shape
     hidden = up.shape[1]
     tiles = chans // 128
-    wide_l = hidden // 4
+    wide_l = hidden // 8
     thin_l = hidden - wide_l
     blocks = rows // 8
     chunk = 8 * cols
@@ -63,7 +63,7 @@
     def hello(device):
         pl.semaphore_signal(barrier, inc=1, device_id=device, device_id_type=MESH)
 
-    near = [pair, sib, crs, (lat, east), (lat, west), at(x, z + 1), at(x, z - 1)]
+    near = [pair, sib, crs, (lat, east), (lat, west), at(x, z + 1), at(x, z - 1), at(x, z + 2), at(x, z - 2)]
     near += [at(x + k, z, y_) for k in range(1, NX) for y_ in (y, 1 - y)]
     for device in near:
         hello(device)
@@ -122,13 +122,16 @@
     def block(d, s):
         return lax.rem(z + (NZ - s if d == 0 else s), NZ)
 
-    def z1(w, d, s):
-        ref = wide(w, block(d, s))
-        return remote(ref, ref, z1_ss.at[w, d, s], z1_rs.at[w, d, s], at(x, z + 1 if d == 0 else z - 1))
-
-    def z2(w, d, s):
-        ref = thin(w, x, block(d, s))
-        return remote(ref, ref, z2_ss.at[w, d, s], z2_rs.at[w, d, s], at(x, z + 1 if d == 0 else z - 1))
+    def z1(w, d, s, j):
+        ref = wide(w, block(d, 2 * s))
+        return remote(ref, ref, z1_ss.at[w, d, s, j], z1_rs.at[w, d, s, j], at(x, z + (1 + j) * (1 - 2 * d)))
+
+    def z2(w, d, s, j):
+        ref = thin(w, x, block(d, 2 * s))
+        return remote(ref, ref, z2_ss.at[w, d, s, j], z2_rs.at[w, d, s, j], at(x, z + (1 + j) * (1 - 2 * d)))
+
+    def reach(w, d, s):
+        return [j for j in (1, 0) if s < HOPS and 2 * s + j < length(w, d)]
 
     def slot_block(d, s, own_slot):
         return jnp.where(own_slot, z, block(d, s + 1)) if not isinstance(own_slot, bool) else (
@@ -191,7 +194,8 @@
     for w in range(2):
         y_copy(w).wait_recv()
         for d in range(2):
-            z2(w, d, 0).start()
+            for j in reach(w, d, 0):
+                z2(w, d, 0, j).start()
         for e in range(2):
             x2(w, e, 1 - w, STEPS - 1, True).start()
     for c in range(2):
@@ -218,21 +222,22 @@
 
     def thin_step(w, s):
         for d in range(2):
-            if isinstance(s, int) and s >= length(w, d):
-                continue
-            z2(w, d, s).wait_recv()
-            if not isinstance(s, int) or s + 1 < length(w, d):
-                z2(w, d, s + 1).start()
-            for e in range(2):
-                x2(w, e, d, s).start()
-            if isinstance(s, int) and s >= DIRECT:
-                xd(w, d, s).start()
-        if isinstance(s, int) and s == 0:
+            for j in reach(w, d, s):
+                z2(w, d, s, j).wait_recv()
+                if j == 1:
+                    for i in reach(w, d, s + 1):
+                        z2(w, d, s + 1, i).start()
+                for e in range(2):
+                    x2(w, e, d, 2 * s + j).start()
+                if 2 * s + j >= DIRECT:
+                    xd(w, d, 2 * s + j).start()
+        if s == 0:
             x2(w, 1 - w, 1 - w, STEPS - 1, True).wait_recv()
             xf(w, 1 - w, STEPS - 1, True).start()
-        elif not isinstance(s, int) or s <= DIRECT:
+        else:
             for d in range(2):
-                cross_step(w, d, s - 1)
+                for j in range(2):
+                    cross_step(w, d, 2 * s - 2 + j)
 
     def cross_step(w, d, s):
         x2(w, d, d, s).wait_recv()
@@ -240,11 +245,11 @@
 
     def wide_step(w, s):
         for d in range(2):
-            if isinstance(s, int) and s >= length(w, d):
-                continue
-            z1(w, d, s).wait_recv()
-            if not isinstance(s, int) or s + 1 < length(w, d):
-                z1(w, d, s + 1).start()
+            for j in reach(w, d, s):
+                z1(w, d, s, j).wait_recv()
+                if j == 1:
+                    for i in reach(w, d, s + 1):
+                        z1(w, d, s + 1, i).start()
 
     def gathered(w):
         for d in range(2):
@@ -263,17 +268,17 @@
             for i in range(2):
                 x1(w, k, i).wait_recv()
         for d in range(2):
-            z1(w, d, 0).start()
+            for j in reach(w, d, 0):
+                z1(w, d, 0, j).start()
     for side in range(2):
         h_copy(side, 2).start()
-    for s in range(EARLY + 1):
-        for w in range(2):
-            thin_step(w, s)
-            if s > 0:
-                wide_step(w, s - 1)
-        if s == 0:
-            for side in range(2):
-                h_copy(side, 3).start()
+    for w in range(2):
+        thin_step(w, 0)
+    for side in range(2):
+        h_copy(side, 3).start()
+    for w in range(2):
+        wide_step(w, 0)
+        thin_step(w, 1)
     for c in loads[2:]:
         c.wait()
 
@@ -347,6 +352,13 @@
     def a_fwd(c):
         return remote(act(far, c), act(far, c), a_ss.at[2, c], a_rs.at[2, c], sib)
 
+    def turn(w, rb):
+        for i, (step, s) in enumerate(((wide_step, 1), (thin_step, 2), (wide_step, 2), (thin_step, 3))):
+
+            @pl.when(rb == i)
+            def _(step=step, s=s):
+                step(w, s)
+
     def conv_block(rb, _):
         @pl.when(rb < blocks - 1)
         def _():
@@ -361,8 +373,7 @@
             return 0
 
         lax.fori_loop(0, tiles // 2, run, 0)
-        thin_step(0, rb + EARLY + 1)
-        wide_step(0, rb + EARLY)
+        turn(0, rb)
         lax.fori_loop(tiles // 2, tiles, run, 0)
 
         def run_norm(g, _):
@@ -372,8 +383,7 @@
         lax.fori_loop(0, chunk // 16, run_norm, 0)
         a_crs(rb).start()
         a_sib(rb).start()
-        thin_step(1, rb + EARLY + 1)
-        wide_step(1, rb + EARLY)
+        turn(1, rb)
         return 0
 
     lax.fori_loop(0, blocks, conv_block, 0)
@@ -382,17 +392,11 @@
         a_crs(c).wait_recv()
         a_fwd(c).start()
 
-    pending = list(range(blocks))
-    for s in range(EARLY + blocks, STEPS + 1):
-        for w in range(2):
-            if s + 1 < STEPS:
-                thin_step(w, s + 1)
-            if s < STEPS:
-                wide_step(w, s)
-            if w == 0 and pending:
-                forward(pending.pop(0))
-    for c in pending:
+    for c in range(blocks - 1):
         forward(c)
+    for w in range(2):
+        wide_step(w, HOPS - 1)
+    forward(blocks - 1)
     gathered(0)
 
     def pointwise(q, h):
@@ -483,12 +487,10 @@
         bulk(w, xf_ss.at[w], xf_rs.at[w]).wait_send()
         for d in range(2):
 
-            def gone(s, _, w=w, d=d):
-                z1(w, d, s).wait_send()
-                z2(w, d, s).wait_send()
-                return 0
-
-            lax.fori_loop(0, length(w, d), gone, 0)
+            for s in range(HOPS):
+                for j in reach(w, d, s):
+                    z1(w, d, s, j).wait_send()
+                    z2(w, d, s, j).wait_send()
     for side in range(2):
         for c in range(blocks):
             h_copy(side, c).wait_send()
@@ -561,8 +563,8 @@
             dma((2, NX - 1, 2)), dma((2, NX - 1, 2)),
             dma((2, 2)), dma((2, 2, 2, STEPS)),
             dma((2,)), dma((2,)),
-            dma((2, 2, STEPS)), dma((2, 2, STEPS)),
-            dma((2, 2, STEPS)), dma((2, 2, STEPS)),
+            dma((2, 2, HOPS, 2)), dma((2, 2, HOPS, 2)),
+            dma((2, 2, HOPS, 2)), dma((2, 2, HOPS, 2)),
             dma((3, blocks)), dma((3, blocks)),
             dma((3, NX)), dma((3, NX)),
         ],

time: 79.9 us -> 80.1 us (level)
  no operation moved by 1% of the time
where the time goes in v4:
time: 80.1 us; the launch traced here: 79.9 us
  Pallas kernels  78.1 us (98%)
  local copies, waits for them, and re-layouts  1.87 us (2%)
    pallas_call x1, Pallas kernels, local(): pl.pallas_call(kernel, out_shape=jax.ShapeDtypeStruct(features.shape, fea...  78.1 us
    unnamed x1, local copies, waits for them, and re-layouts  1.87 us

profile of v4, /device:TPU:1, one launch (start us, length us, event | category | flops | bytes accessed | tf_op | source)
XLA Modules:
  0.0 79.9 jit_solution(17278248368361521205)
XLA Ops:
  0.0 78.1 %shard_map.100 = bf16[32,8,1024]{2,1,0:T(8,128)(2,1)} custom-call(bf16[32,8,1024]{2,1,0:T(8,128)(2,1)} %feat_h.1, bf16[7,7,1024]{2,1,0:T(8,128)(2,1)} %dker_h.1, f32[1,1024]{1,0:T(1,128)} %bitcast.6, f32[1,1024]{1,0:T(1,128)} %bitcast.7, f32[1,1024]{1,0:T(1,128)} %bitcast.8, bf16[8,1024]{1,0:T(8,128)(2,1)} %up.1, f32[1,1024]{1,0:T(1,128)} %bitcast.9, ...), custom_call_target="tpu_custom_call" | custom-call | tf_op jit(solution)/shard_map/pallas_call | solution.py:529
  78.1 1.9 %copy.12 = bf16[32,8,1024]{2,1,0:T(8,128)(2,1)} copy(bf16[32,8,1024]{2,1,0:T(8,128)(2,1)} %shard_map.100) | data formatting | bytes 1048576

commit v5 on v3

--- a/solution.py
+++ b/solution.py
@@ -31,7 +31,7 @@
     rows, cols, chans = feat.shape
     hidden = up.shape[1]
     tiles = chans // 128
-    wide_l = hidden // 4
+    wide_l = hidden // 8
     thin_l = hidden - wide_l
     blocks = rows // 8
     chunk = 8 * cols

time: 79.9 us -> 82.2 us (1.029)
  Pallas kernels: 77.9 us -> 80.2 us
    pallas_call x1, Pallas kernels: 77.9 us -> 80.2 us  [local(): pl.pallas_call(kernel, out_shape=jax.ShapeDtypeStruct(features.shape, fea...]
where the time goes in v5:
time: 82.2 us; the launch traced here: 82 us
  Pallas kernels  80.2 us (98%)
  local copies, waits for them, and re-layouts  1.87 us (2%)
    pallas_call x1, Pallas kernels, local(): pl.pallas_call(kernel, out_shape=jax.ShapeDtypeStruct(features.shape, fea...  80.2 us
    unnamed x1, local copies, waits for them, and re-layouts  1.87 us

profile of v5, /device:TPU:1, one launch (start us, length us, event | category | flops | bytes accessed | tf_op | source)
XLA Modules:
  0.0 82.0 jit_solution(10466307972190828703)
XLA Ops:
  0.0 80.2 %shard_map.100 = bf16[32,8,1024]{2,1,0:T(8,128)(2,1)} custom-call(bf16[32,8,1024]{2,1,0:T(8,128)(2,1)} %feat_h.1, bf16[7,7,1024]{2,1,0:T(8,128)(2,1)} %dker_h.1, f32[1,1024]{1,0:T(1,128)} %bitcast.6, f32[1,1024]{1,0:T(1,128)} %bitcast.7, f32[1,1024]{1,0:T(1,128)} %bitcast.8, bf16[8,1024]{1,0:T(8,128)(2,1)} %up.1, f32[1,1024]{1,0:T(1,128)} %bitcast.9, ...), custom_call_target="tpu_custom_call" | custom-call | tf_op jit(solution)/shard_map/pallas_call | solution.py:527
  80.2 1.9 %copy.12 = bf16[32,8,1024]{2,1,0:T(8,128)(2,1)} copy(bf16[32,8,1024]{2,1,0:T(8,128)(2,1)} %shard_map.100) | data formatting | bytes 1048576
